TPU v7x, 32 devices: a whole 2x2x4 slice. The times are simulated.
32 devices in a mesh: pair: 2 (over core), vcol: 16 (over z, y, x).
Axes of the slice: x: 2, y: 2, z: 4, core: 2. Of those that a mesh axis runs over, the one named last changes fastest.
Arguments:
- amplitudes: bfloat16 [1280, 4096], P('pair', 'vcol'), may hold values from -6 to 6
- tile_owner: int32 [32], replicated, may hold values from 0 to 31, each once
- integrals: bfloat16 [4096, 4096], P('pair', 'vcol'), may hold values from -0.125 to 0.125
- screening: int32 [20, 32, 32], P('pair'), may hold values 0 or 1
- occ_energy: float32 [1280], P('pair'), may hold values from -1 to -0.2
- virt_energy: float32 [4096], replicated, may hold values from 0.2 to 1
Outputs:
- residual: bfloat16 [1280, 4096], P('pair', 'vcol')
Inputs may be any that keep to these rules, and one draw needn't show every extreme that they name: `tile_owner`: each of the 32 tiles appears exactly once.
All inputs are finite; a program needn't handle non-finite values. No bound on the sum of `screening` on one device may be relied on, other than what follows from the above.
Results may differ from a plain program's by a relative error of at most 0.0036.
Values may be sent and summed in bfloat16 or wider, within the bound.
A program may use at most 64 MiB of HBM per device.

v0:
```python
import jax
import jax.numpy as jnp
from jax import lax
from jax.sharding import PartitionSpec as P

TILE = 128
PBLK = 64
KT_DEV = 2


def one_hot(indices, length):
    return (indices[:, None] == jnp.arange(length, dtype=jnp.int32)[None, :]).astype(jnp.float32)


def gather_rows(panel):
    return lax.all_gather(panel, "pair", axis=0, tiled=True)


def local(amplitudes, tile_owner, integrals, screening, occ_energy, virt_energy):
    pair_local = amplitudes.shape[0]
    tile_count = tile_owner.shape[0]
    width = KT_DEV * TILE
    block_count = pair_local // PBLK
    column = lax.axis_index("vcol")
    first_slot = column * KT_DEV
    owned_tiles = lax.dynamic_slice_in_dim(tile_owner, first_slot, KT_DEV, 0)
    screen_float = screening.astype(jnp.float32)
    natural_tiles = first_slot + jnp.arange(KT_DEV, dtype=jnp.int32)
    panel = gather_rows(integrals)
    picked = jnp.einsum("bct,jt->bcj", screen_float, one_hot(natural_tiles, tile_count))
    marks_slot = jnp.take(picked, tile_owner, axis=1).astype(jnp.bfloat16)
    panel_slot = jnp.take(panel.reshape(tile_count, TILE, width), tile_owner, axis=0)
    piece_in = lax.all_gather(amplitudes, "vcol", axis=1, tiled=True)
    tiles_in = piece_in.shape[1] // TILE
    left_all = piece_in.reshape(block_count, PBLK, tiles_in * TILE)

    def one_block(operands):
        left_rows, marks = operands
        masked = (
            panel_slot.reshape(tiles_in, TILE, KT_DEV, TILE) * marks[:, None, :, None]
        ).reshape(tiles_in * TILE, width)
        return jnp.dot(left_rows, masked, preferred_element_type=jnp.float32)

    summed = lax.map(one_block, (left_all, marks_slot))
    ladder_local = summed.reshape(pair_local, width).astype(jnp.bfloat16)
    ranks = tile_count // KT_DEV
    rows = pair_local // ranks
    parts = ladder_local.reshape(ranks, rows, KT_DEV, TILE).transpose(0, 2, 1, 3)
    spread = lax.all_to_all(parts, "vcol", 0, 0, tiled=True).reshape(tile_count, rows, TILE)
    by_slot = jnp.take(spread, tile_owner, axis=0).reshape(ranks, KT_DEV, rows, TILE)
    back = lax.all_to_all(by_slot, "vcol", 0, 0, tiled=True)
    ladder_owned = back.transpose(0, 2, 1, 3).reshape(pair_local, width).astype(jnp.float32)
    virt_owned = jnp.dot(
        one_hot(owned_tiles, tile_count),
        virt_energy.reshape(tile_count, TILE),
        precision=lax.Precision.HIGHEST,
    ).reshape(width)
    residual = ladder_owned + (virt_owned[None, :] - occ_energy[:, None]) * amplitudes.astype(
        jnp.float32
    )
    return residual.astype(jnp.bfloat16)


def solution(mesh):
    return jax.shard_map(
        local,
        mesh=mesh,
        in_specs=(P("pair", "vcol"), P(), P("pair", "vcol"), P("pair", None, None), P("pair"), P()),
        out_specs=P("pair", "vcol"),
        check_vma=False,
    )
```

profile of v0, /device:TPU:0, one launch (start us, length us, event | category | flops | bytes accessed | tf_op | source)
XLA Modules:
  0.0 183.6 jit_solution(1509187314705847250)
XLA Ops:
  6.5 0.7 all-gather.5.cloned.1.call-update
  7.3 0.7 all-gather.3.cloned.1.call-update
  8.0 1.2 convolution_bitcast_fusion.1
  9.3 0.7 compare_select_fusion
  10.0 0.6 gather_fusion
  10.6 0.7 compare_and_fusion
  11.5 10.7 %all-gather.5.cloned.1.call-done = bf16[4096,256]{1,0:T(8,128)(2,1)} async-done(((bf16[2048,256]{1,0:T(8,128)(2,1)}), bf16[4096,256]{1,0:T(8,128)(2,1)}) %all-gather.5.cloned.1.call-update) | async-done | bytes 2097168 | tf_op jit(solution)/shard_map/all_gather | solution.py:16
  22.2 3.7 %gather_fusion.1 = bf16[32,128,256]{2,1,0:T(8,128)(2,1)} fusion(bf16[32,128,256]{2,1,0:T(8,128)(2,1)} %bitcast.56, s32[1024]{0:T(1024)S(1)} %pad_clamp_fusion), kind=kCustom, calls=%fused_computation.1 | custom fusion | bytes 4194432 | tf_op jit(solution)/shard_map/jit(_take)/gather | solution.py:32
  25.9 1.8 %broadcast_select_fusion = bf16[32,128,256]{2,1,0:T(8,128)(2,1)S(1)} fusion(bf16[32,128,256]{2,1,0:T(8,128)(2,1)} %gather_fusion.1, pred[32]{0:T(512)(128)(4,1)S(1)} %compare_and_fusion), kind=kLoop, calls=%fused_computation.12 | loop fusion | flops 1048576 | bytes 4194336 | tf_op jit(solution)/shard_map/jit(_take)/select_n | solution.py:32
  27.7 96.8 %all-gather.3.cloned.1.call-done = bf16[640,4096]{1,0:T(8,128)(2,1)} async-done(((bf16[640,256]{1,0:T(8,128)(2,1)}), bf16[640,4096]{1,0:T(8,128)(2,1)}) %all-gather.3.cloned.1.call-update) | async-done | bytes 5242896 | tf_op jit(solution)/shard_map/all_gather | solution.py:33
  124.5 19.2 %while.10 = (s32[]{:T(128)}, bf16[10,64,256]{2,1,0:T(8,128)(2,1)S(1)}, bf16[10,64,4096]{2,1,0:T(8,128)(2,1)}, bf16[10,32,2]{1,2,0:T(2,128)(2,1)S(1)}, bf16[32,128,256]{2,1,0:T(8,128)(2,1)S(1)}, /*index=5*/s32[]{:T(128)}) while((s32[]{:T(128)}, bf16[10,64,256]{2,1,0:T(8,128)(2,1)S(1)}, bf16[10,64,4096]{2,1,0:T(8,128)(2,1)}, ...), condition=%wide.region_1.2_spmd, body=%wide.region_0.1_spmd.sunk | while | flops 135266304 | bytes 6948553 | solution.py:44
  124.9 1.5 fusion.24
  126.7 0.1 broadcast_multiply_fusion.2
  126.8 1.5 fusion.24
  128.7 1.5 fusion.24
  130.7 1.5 fusion.24
  132.6 1.5 fusion.24
  134.5 1.5 fusion.24
  136.4 1.5 fusion.24
  138.4 1.5 fusion.24
  140.3 1.5 fusion.24
  142.2 1.5 fusion.24
  143.7 0.8 convert_element_type.33
  144.5 3.8 %all-to-all-start = ((bf16[16,2,40,128]{3,1,2,0:T(2,128)(2,1)}), bf16[16,2,40,128]{3,1,2,0:T(2,128)(2,1)S(1)}, u32[]{:S(2)}, u32[]{:S(2)}) async-start(bf16[16,2,40,128]{3,1,2,0:T(2,128)(2,1)} %bitcast.9), calls=%async_computation | async-start | bytes 655360 | tf_op jit(solution)/shard_map/all_to_all | solution.py:49
  148.4 11.2 %all-to-all-done = bf16[16,2,40,128]{3,1,2,0:T(2,128)(2,1)S(1)} async-done(((bf16[16,2,40,128]{3,1,2,0:T(2,128)(2,1)}), bf16[16,2,40,128]{3,1,2,0:T(2,128)(2,1)S(1)}, u32[]{:S(2)}, u32[]{:S(2)}) %all-to-all-start) | async-done | bytes 327712 | tf_op jit(solution)/shard_map/all_to_all | solution.py:49
  159.7 0.6 gather_fusion.2
  160.4 0.8 broadcast_select_fusion.1
  161.2 3.5 %all-to-all-start.1 = ((bf16[16,2,40,128]{3,2,1,0:T(8,128)(2,1)}), bf16[16,2,40,128]{3,2,1,0:T(8,128)(2,1)S(1)}, u32[]{:S(2)}, u32[]{:S(2)}) async-start(bf16[16,2,40,128]{3,2,1,0:T(8,128)(2,1)} %broadcast_select_fusion.1), calls=%async_computation.1 | async-start | bytes 655360 | tf_op jit(solution)/shard_map/all_to_all | solution.py:51
  164.8 0.2 convolution_bitcast_fusion.2
  165.0 10.4 %all-to-all-done.1 = bf16[16,2,40,128]{3,2,1,0:T(8,128)(2,1)S(1)} async-done(((bf16[16,2,40,128]{3,2,1,0:T(8,128)(2,1)}), bf16[16,2,40,128]{3,2,1,0:T(8,128)(2,1)S(1)}, u32[]{:S(2)}, u32[]{:S(2)}) %all-to-all-start.1) | async-done | bytes 327712 | tf_op jit(solution)/shard_map/all_to_all | solution.py:51
  175.5 0.3 copy.15
  175.9 0.9 fusion.5
  (69 shorter events, 4.1 us)
Async XLA Ops:
  6.5 158.3 %copy-start = (f32[4096]{0:T(1024)S(1)}, f32[4096]{0:T(1024)}, u32[]{:S(2)}) copy-start(f32[4096]{0:T(1024)} %param.13) | copy-start | bytes 49156
  6.5 15.7 %all-gather.5.cloned.1.call-start = ((), (), s32[]{:S(2)}) async-start(), calls=%async_computation.3 | async-start | bytes 3145728 | tf_op jit(solution)/shard_map/all_gather | solution.py:16
  7.3 117.2 %all-gather.3.cloned.1.call-start = ((), (), s32[]{:S(2)}) async-start(), calls=%async_computation.2 | async-start | bytes 5570560 | tf_op jit(solution)/shard_map/all_gather | solution.py:33
  143.7 21.0 %copy-start.3 = (s32[32]{0:T(128)S(1)}, s32[32]{0:T(128)}, u32[]{:S(2)}) copy-start(s32[32]{0:T(128)} %param.9) | copy-start | bytes 388
  144.5 15.1 %all-to-all-start = ((bf16[16,2,40,128]{3,1,2,0:T(2,128)(2,1)}), bf16[16,2,40,128]{3,1,2,0:T(2,128)(2,1)S(1)}, u32[]{:S(2)}, u32[]{:S(2)}) async-start(bf16[16,2,40,128]{3,1,2,0:T(2,128)(2,1)} %bitcast.9), calls=%async_computation | async-start | bytes 655360 | tf_op jit(solution)/shard_map/all_to_all | solution.py:49
  159.7 16.1 %copy-start.1 = (bf16[640,256]{1,0:T(8,128)(2,1)S(1)}, bf16[640,256]{1,0:T(8,128)(2,1)}, u32[]{:S(2)}) copy-start(bf16[640,256]{1,0:T(8,128)(2,1)} %param.8) | copy-start | bytes 983044
  159.7 16.1 %copy-start.2 = (f32[640]{0:T(1024)S(1)}, f32[640]{0:T(1024)}, u32[]{:S(2)}) copy-start(f32[640]{0:T(1024)} %param.12) | copy-start | bytes 7684
  161.2 14.3 %all-to-all-start.1 = ((bf16[16,2,40,128]{3,2,1,0:T(8,128)(2,1)}), bf16[16,2,40,128]{3,2,1,0:T(8,128)(2,1)S(1)}, u32[]{:S(2)}, u32[]{:S(2)}) async-start(bf16[16,2,40,128]{3,2,1,0:T(8,128)(2,1)} %broadcast_select_fusion.1), calls=%async_computation.1 | async-start | bytes 655360 | tf_op jit(solution)/shard_map/all_to_all | solution.py:51
Sparse Core Ops, SparseCore 0:
  8.9 13.2 all-gather.4
  24.9 99.5 all-gather.2
where the time goes:
time: 185 us; the launch traced here: 184 us
  waiting for transfers between devices  131 us (71%)
  matrix products  16.5 us (9%)
  between operations  13.5 us (7%)
  local copies, waits for them, and re-layouts  8.64 us (5%)
  starting transfers between devices  7.39 us (4%)
  other arithmetic  6.53 us (4%)
    all_gather x1, waiting for transfers between devices, local(): piece_in = lax.all_gather(amplitudes, 'vcol', axis=1, tiled=True)  96.8 us
    dot_general x10, matrix products, one_block(): return jnp.dot(left_rows, masked, preferred_element_type=jnp.float32)  15.1 us
    all_to_all x1, waiting for transfers between devices, local(): lax.all_to_all(parts, 'vcol', 0, 0, tiled=True)  11.2 us
    all_gather x1, waiting for transfers between devices, gather_rows(): return lax.all_gather(panel, 'pair', axis=0, tiled=True)  10.7 us
    all_to_all x1, waiting for transfers between devices, local(): back = lax.all_to_all(by_slot, 'vcol', 0, 0, tiled=True)  10.4 us
    all_to_all x1, starting transfers between devices, local(): lax.all_to_all(parts, 'vcol', 0, 0, tiled=True)  3.8 us
  transfers between devices with their start and end apart: 4, of which 4 were waited for; matrix products, arithmetic and copies ran while one was open for 5% of the time, Pallas kernels for 0%

commit v1 on v0

--- a/solution.py
+++ b/solution.py
@@ -6,6 +6,18 @@
 TILE = 128
 PBLK = 64
 KT_DEV = 2
+
+
+def _unite_teams(sample, array_axis, mat):
+    u1, now = (sample.shape[:array_axis], sample.shape[array_axis + 1 :])
+    p_next = sample.reshape(*u1, mat, -1, *now)
+    return jnp.moveaxis(p_next, array_axis, 0)
+
+
+def drive_rows(chunk, d_out):
+    chunk = jnp.moveaxis(chunk, 0, d_out)
+    t_next = chunk.shape
+    return chunk.reshape(*t_next[:d_out], t_next[d_out] * t_next[d_out + 1], *t_next[d_out + 2 :])
 
 
 def one_hot(indices, length):
@@ -48,7 +60,18 @@
     parts = ladder_local.reshape(ranks, rows, KT_DEV, TILE).transpose(0, 2, 1, 3)
     spread = lax.all_to_all(parts, "vcol", 0, 0, tiled=True).reshape(tile_count, rows, TILE)
     by_slot = jnp.take(spread, tile_owner, axis=0).reshape(ranks, KT_DEV, rows, TILE)
-    back = lax.all_to_all(by_slot, "vcol", 0, 0, tiled=True)
+    block_now = lax.psum(1, "vcol")
+    next_value = lax.axis_index("vcol")
+    oldest, moved = (block_now, next_value)
+    carry_in = _unite_teams(by_slot, 0, oldest)
+    grid = [carry_in[moved]]
+    for nth in range(1, oldest):
+        later = carry_in[moved ^ nth]
+        f_now = lax.ppermute(later, "vcol", [(t, t ^ nth) for t in range(oldest)])
+        grid.append(f_now)
+    all_rows = jnp.stack(grid)
+    carry_in = all_rows[moved ^ jnp.arange(oldest)]
+    back = drive_rows(carry_in, 0)
     ladder_owned = back.transpose(0, 2, 1, 3).reshape(pair_local, width).astype(jnp.float32)
     virt_owned = jnp.dot(
         one_hot(owned_tiles, tile_count),

time: 185 us -> 201 us (1.086)
  starting transfers between devices: 7.39 us -> 30.9 us
  waiting for transfers between devices: 131 us -> 124 us
    ppermute x0 -> x15, starting transfers between devices: none -> 27.1 us  [local(): f_now = lax.ppermute(later, 'vcol', [(t, t ^ nth) for t in range(oldest)])]
    all_to_all x1 -> x0, waiting for transfers between devices: 10.4 us -> none  [local(): back = lax.all_to_all(by_slot, 'vcol', 0, 0, tiled=True)]
    ppermute x0 -> x15, waiting for transfers between devices: none -> 3.82 us  [local(): f_now = lax.ppermute(later, 'vcol', [(t, t ^ nth) for t in range(oldest)])]
    all_to_all x1 -> x0, starting transfers between devices: 3.54 us -> none  [local(): back = lax.all_to_all(by_slot, 'vcol', 0, 0, tiled=True)]
  transfers between devices with their start and end apart: 4 -> 18, of which waited for: 4 -> 5; matrix products, arithmetic and copies ran while one was open for 5% -> 5% of each run, Pallas kernels for 0% -> 0%
where the time goes in v1:
time: 201 us; the launch traced here: 200 us
  waiting for transfers between devices  124 us (62%)
  starting transfers between devices  30.9 us (15%)
  matrix products  16.5 us (8%)
  between operations  13.7 us (7%)
  local copies, waits for them, and re-layouts  9.51 us (5%)
  other arithmetic  5.82 us (3%)
    all_gather x1, waiting for transfers between devices, local(): piece_in = lax.all_gather(amplitudes, 'vcol', axis=1, tiled=True)  96.8 us
    ppermute x15, starting transfers between devices, local(): f_now = lax.ppermute(later, 'vcol', [(t, t ^ nth) for t in range(oldest)])  27.1 us
    dot_general x10, matrix products, one_block(): return jnp.dot(left_rows, masked, preferred_element_type=jnp.float32)  15.1 us
    all_to_all x1, waiting for transfers between devices, local(): lax.all_to_all(parts, 'vcol', 0, 0, tiled=True)  10.8 us
    all_gather x1, waiting for transfers between devices, gather_rows(): return lax.all_gather(panel, 'pair', axis=0, tiled=True)  10.7 us
  transfers between devices with their start and end apart: 18, of which 5 were waited for; matrix products, arithmetic and copies ran while one was open for 5% of the time, Pallas kernels for 0%

profile of v1, /device:TPU:0, one launch (start us, length us, event | category | flops | bytes accessed | tf_op | source)
XLA Modules:
  0.0 200.5 jit_solution(15925326912701044223)
XLA Ops:
  8.0 1.2 convolution_bitcast_fusion.1
  11.5 10.7 %all-gather.5.cloned.1.call-done = bf16[4096,256]{1,0:T(8,128)(2,1)} async-done(((bf16[2048,256]{1,0:T(8,128)(2,1)}), bf16[4096,256]{1,0:T(8,128)(2,1)}) %all-gather.5.cloned.1.call-update) | async-done | bytes 2097168 | tf_op jit(solution)/shard_map/all_gather | solution.py:28
  22.2 3.7 %gather_fusion.1 = bf16[32,128,256]{2,1,0:T(8,128)(2,1)} fusion(bf16[32,128,256]{2,1,0:T(8,128)(2,1)} %bitcast.119, s32[1024]{0:T(1024)S(1)} %pad_clamp_fusion.1), kind=kCustom, calls=%fused_computation.1 | custom fusion | bytes 4194432 | tf_op jit(solution)/shard_map/jit(_take)/gather | solution.py:44
  25.9 1.8 broadcast_select_fusion
  27.7 96.8 %all-gather.3.cloned.1.call-done = bf16[640,4096]{1,0:T(8,128)(2,1)} async-done(((bf16[640,256]{1,0:T(8,128)(2,1)}), bf16[640,4096]{1,0:T(8,128)(2,1)}) %all-gather.3.cloned.1.call-update) | async-done | bytes 5242896 | tf_op jit(solution)/shard_map/all_gather | solution.py:45
  124.5 19.2 %while.10 = (s32[]{:T(128)}, bf16[10,64,256]{2,1,0:T(8,128)(2,1)S(1)}, bf16[10,64,4096]{2,1,0:T(8,128)(2,1)}, bf16[10,32,2]{1,2,0:T(2,128)(2,1)S(1)}, bf16[32,128,256]{2,1,0:T(8,128)(2,1)S(1)}, /*index=5*/s32[]{:T(128)}) while((s32[]{:T(128)}, bf16[10,64,256]{2,1,0:T(8,128)(2,1)S(1)}, bf16[10,64,4096]{2,1,0:T(8,128)(2,1)}, ...), condition=%wide.region_1.2_spmd, body=%wide.region_0.1_spmd.sunk | while | flops 135266304 | bytes 6948561 | solution.py:56
  124.9 1.5 fusion.25
  126.8 1.5 fusion.25
  128.7 1.5 fusion.25
  130.7 1.5 fusion.25
  132.6 1.5 fusion.25
  134.5 1.5 fusion.25
  136.4 1.5 fusion.25
  138.4 1.5 fusion.25
  140.3 1.5 fusion.25
  142.2 1.5 fusion.25
  144.5 3.8 %all-to-all-start = ((bf16[16,2,40,128]{3,1,2,0:T(2,128)(2,1)}), bf16[16,2,40,128]{3,1,2,0:T(2,128)(2,1)S(1)}, u32[]{:S(2)}, u32[]{:S(2)}) async-start(bf16[16,2,40,128]{3,1,2,0:T(2,128)(2,1)} %bitcast.9), calls=%async_computation | async-start | bytes 655360 | tf_op jit(solution)/shard_map/all_to_all | solution.py:61
  148.8 10.8 %all-to-all-done = bf16[16,2,40,128]{3,1,2,0:T(2,128)(2,1)S(1)} async-done(((bf16[16,2,40,128]{3,1,2,0:T(2,128)(2,1)}), bf16[16,2,40,128]{3,1,2,0:T(2,128)(2,1)S(1)}, u32[]{:S(2)}, u32[]{:S(2)}) %all-to-all-start) | async-done | bytes 327712 | tf_op jit(solution)/shard_map/all_to_all | solution.py:61
  162.0 2.1 %collective-permute-start.2 = (bf16[1,2,40,128]{3,2,1,0:T(8,128)(2,1)S(1)}, bf16[1,2,40,128]{3,2,1,0:T(8,128)(2,1)S(1)}, u32[]{:S(2)}, u32[]{:S(2)}) collective-permute-start(bf16[1,2,40,128]{3,2,1,0:T(8,128)(2,1)S(1)} %get-tuple-element.65), channel_id=1, source_target_pairs={{0,3},{1,2},{2,1},{3,0},{4,7},{5,6},{6,5},{7,4},{8,11},{9,10},{10,... | collective-permute-start | bytes 61448 | tf_op jit(solution)/shard_map/ppermute | solution.py:70
  164.2 1.0 collective-permute-start.3
  165.2 1.0 collective-permute-start.4
  166.2 1.2 collective-permute-start.5
  167.4 2.7 %collective-permute-start.6 = (bf16[1,2,40,128]{3,2,1,0:T(8,128)(2,1)S(1)}, bf16[1,2,40,128]{3,2,1,0:T(8,128)(2,1)S(1)}, u32[]{:S(2)}, u32[]{:S(2)}) collective-permute-start(bf16[1,2,40,128]{3,2,1,0:T(8,128)(2,1)S(1)} %get-tuple-element.61), channel_id=1, source_target_pairs={{0,7},{1,6},{2,5},{3,4},{4,3},{5,2},{6,1},{7,0},{8,15},{9,14},{10,... | collective-permute-start | bytes 61448 | tf_op jit(solution)/shard_map/ppermute | solution.py:70
  170.5 2.7 %collective-permute-start.8 = (bf16[1,2,40,128]{3,2,1,0:T(8,128)(2,1)S(1)}, bf16[1,2,40,128]{3,2,1,0:T(8,128)(2,1)S(1)}, u32[]{:S(2)}, u32[]{:S(2)}) collective-permute-start(bf16[1,2,40,128]{3,2,1,0:T(8,128)(2,1)S(1)} %get-tuple-element.59), channel_id=1, source_target_pairs={{0,9},{1,8},{2,11},{3,10},{4,13},{5,12},{6,15},{7,14},{8,1},{9,0},... | collective-permute-start | bytes 61448 | tf_op jit(solution)/shard_map/ppermute | solution.py:70
  173.2 0.9 collective-permute-start.9
  174.1 4.0 %collective-permute-start.10 = (bf16[1,2,40,128]{3,2,1,0:T(8,128)(2,1)S(1)}, bf16[1,2,40,128]{3,2,1,0:T(8,128)(2,1)S(1)}, u32[]{:S(2)}, u32[]{:S(2)}) collective-permute-start(bf16[1,2,40,128]{3,2,1,0:T(8,128)(2,1)S(1)} %get-tuple-element.57), channel_id=1, source_target_pairs={{0,11},{1,10},{2,9},{3,8},{4,15},{5,14},{6,13},{7,12},{8,3},{9,2},... | collective-permute-start | bytes 61448 | tf_op jit(solution)/shard_map/ppermute | solution.py:70
  178.1 1.7 collective-permute-start.11
  179.8 2.2 %collective-permute-start.12 = (bf16[1,2,40,128]{3,2,1,0:T(8,128)(2,1)S(1)}, bf16[1,2,40,128]{3,2,1,0:T(8,128)(2,1)S(1)}, u32[]{:S(2)}, u32[]{:S(2)}) collective-permute-start(bf16[1,2,40,128]{3,2,1,0:T(8,128)(2,1)S(1)} %get-tuple-element.55), channel_id=1, source_target_pairs={{0,13},{1,12},{2,15},{3,14},{4,9},{5,8},{6,11},{7,10},{8,5},{9,4},... | collective-permute-start | bytes 61448 | tf_op jit(solution)/shard_map/ppermute | solution.py:70
  182.0 2.2 %collective-permute-start.13 = (bf16[1,2,40,128]{3,2,1,0:T(8,128)(2,1)S(1)}, bf16[1,2,40,128]{3,2,1,0:T(8,128)(2,1)S(1)}, u32[]{:S(2)}, u32[]{:S(2)}) collective-permute-start(bf16[1,2,40,128]{3,2,1,0:T(8,128)(2,1)S(1)} %get-tuple-element.54), channel_id=1, source_target_pairs={{0,14},{1,15},{2,12},{3,13},{4,10},{5,11},{6,8},{7,9},{8,6},{9,7},... | collective-permute-start | bytes 61448 | tf_op jit(solution)/shard_map/ppermute | solution.py:70
  184.2 3.6 %collective-permute-start.14 = (bf16[1,2,40,128]{3,2,1,0:T(8,128)(2,1)S(1)}, bf16[1,2,40,128]{3,2,1,0:T(8,128)(2,1)S(1)}, u32[]{:S(2)}, u32[]{:S(2)}) collective-permute-start(bf16[1,2,40,128]{3,2,1,0:T(8,128)(2,1)S(1)} %get-tuple-element.53), channel_id=1, source_target_pairs={{0,15},{1,14},{2,13},{3,12},{4,11},{5,10},{6,9},{7,8},{8,7},{9,6},... | collective-permute-start | bytes 61448 | tf_op jit(solution)/shard_map/ppermute | solution.py:70
  188.6 3.1 %collective-permute-done.14 = bf16[1,2,40,128]{3,2,1,0:T(8,128)(2,1)S(1)} collective-permute-done((bf16[1,2,40,128]{3,2,1,0:T(8,128)(2,1)S(1)}, bf16[1,2,40,128]{3,2,1,0:T(8,128)(2,1)S(1)}, u32[]{:S(2)}, u32[]{:S(2)}) %collective-permute-start.14) | collective-permute-done | bytes 20512 | tf_op jit(solution)/shard_map/ppermute | solution.py:70
  192.7 0.9 fusion.5
  (116 shorter events, 13.1 us)
Async XLA Ops:
  6.5 142.1 %copy-start = (f32[4096]{0:T(1024)S(1)}, f32[4096]{0:T(1024)}, u32[]{:S(2)}) copy-start(f32[4096]{0:T(1024)} %param.13) | copy-start | bytes 49156
  6.5 15.7 %all-gather.5.cloned.1.call-start = ((), (), s32[]{:S(2)}) async-start(), calls=%async_computation.2 | async-start | bytes 3145728 | tf_op jit(solution)/shard_map/all_gather | solution.py:28
  7.3 117.2 %all-gather.3.cloned.1.call-start = ((), (), s32[]{:S(2)}) async-start(), calls=%async_computation.1 | async-start | bytes 5570560 | tf_op jit(solution)/shard_map/all_gather | solution.py:45
  124.5 24.0 %copy-start.3 = (s32[32]{0:T(128)S(1)}, s32[32]{0:T(128)}, u32[]{:S(2)}) copy-start(s32[32]{0:T(128)} %param.9) | copy-start | bytes 388
  144.5 15.1 %all-to-all-start = ((bf16[16,2,40,128]{3,1,2,0:T(2,128)(2,1)}), bf16[16,2,40,128]{3,1,2,0:T(2,128)(2,1)S(1)}, u32[]{:S(2)}, u32[]{:S(2)}) async-start(bf16[16,2,40,128]{3,1,2,0:T(2,128)(2,1)} %bitcast.9), calls=%async_computation | async-start | bytes 655360 | tf_op jit(solution)/shard_map/all_to_all | solution.py:61
  160.5 32.3 %copy-start.1 = (bf16[640,256]{1,0:T(8,128)(2,1)S(1)}, bf16[640,256]{1,0:T(8,128)(2,1)}, u32[]{:S(2)}) copy-start(bf16[640,256]{1,0:T(8,128)(2,1)} %param.8) | copy-start | bytes 983044
  160.5 32.3 %copy-start.2 = (f32[640]{0:T(1024)S(1)}, f32[640]{0:T(1024)}, u32[]{:S(2)}) copy-start(f32[640]{0:T(1024)} %param.12) | copy-start | bytes 7684
  160.6 5.6 %collective-permute-start = (bf16[1,2,40,128]{3,2,1,0:T(8,128)(2,1)S(1)}, bf16[1,2,40,128]{3,2,1,0:T(8,128)(2,1)S(1)}, u32[]{:S(2)}, u32[]{:S(2)}) collective-permute-start(bf16[1,2,40,128]{3,2,1,0:T(8,128)(2,1)S(1)} %get-tuple-element.67), channel_id=1, source_target_pairs={{0,1},{1,0},{2,3},{3,2},{4,5},{5,4},{6,7},{7,6},{8,9},{9,8},{10,11... | collective-permute-start | bytes 61448 | tf_op jit(solution)/shard_map/ppermute | solution.py:70
  161.2 6.2 %collective-permute-start.1 = (bf16[1,2,40,128]{3,2,1,0:T(8,128)(2,1)S(1)}, bf16[1,2,40,128]{3,2,1,0:T(8,128)(2,1)S(1)}, u32[]{:S(2)}, u32[]{:S(2)}) collective-permute-start(bf16[1,2,40,128]{3,2,1,0:T(8,128)(2,1)S(1)} %get-tuple-element.66), channel_id=1, source_target_pairs={{0,2},{1,3},{2,0},{3,1},{4,6},{5,7},{6,4},{7,5},{8,10},{9,11},{10,... | collective-permute-start | bytes 61448 | tf_op jit(solution)/shard_map/ppermute | solution.py:70
  162.0 8.1 %collective-permute-start.2 = (bf16[1,2,40,128]{3,2,1,0:T(8,128)(2,1)S(1)}, bf16[1,2,40,128]{3,2,1,0:T(8,128)(2,1)S(1)}, u32[]{:S(2)}, u32[]{:S(2)}) collective-permute-start(bf16[1,2,40,128]{3,2,1,0:T(8,128)(2,1)S(1)} %get-tuple-element.65), channel_id=1, source_target_pairs={{0,3},{1,2},{2,1},{3,0},{4,7},{5,6},{6,5},{7,4},{8,11},{9,10},{10,... | collective-permute-start | bytes 61448 | tf_op jit(solution)/shard_map/ppermute | solution.py:70
  164.2 6.3 %collective-permute-start.3 = (bf16[1,2,40,128]{3,2,1,0:T(8,128)(2,1)S(1)}, bf16[1,2,40,128]{3,2,1,0:T(8,128)(2,1)S(1)}, u32[]{:S(2)}, u32[]{:S(2)}) collective-permute-start(bf16[1,2,40,128]{3,2,1,0:T(8,128)(2,1)S(1)} %get-tuple-element.64), channel_id=1, source_target_pairs={{0,4},{1,5},{2,6},{3,7},{4,0},{5,1},{6,2},{7,3},{8,12},{9,13},{10,... | collective-permute-start | bytes 61448 | tf_op jit(solution)/shard_map/ppermute | solution.py:70
  165.2 8.0 %collective-permute-start.4 = (bf16[1,2,40,128]{3,2,1,0:T(8,128)(2,1)S(1)}, bf16[1,2,40,128]{3,2,1,0:T(8,128)(2,1)S(1)}, u32[]{:S(2)}, u32[]{:S(2)}) collective-permute-start(bf16[1,2,40,128]{3,2,1,0:T(8,128)(2,1)S(1)} %get-tuple-element.63), channel_id=1, source_target_pairs={{0,5},{1,4},{2,7},{3,6},{4,1},{5,0},{6,3},{7,2},{8,13},{9,12},{10,... | collective-permute-start | bytes 61448 | tf_op jit(solution)/shard_map/ppermute | solution.py:70
  166.2 7.9 %collective-permute-start.5 = (bf16[1,2,40,128]{3,2,1,0:T(8,128)(2,1)S(1)}, bf16[1,2,40,128]{3,2,1,0:T(8,128)(2,1)S(1)}, u32[]{:S(2)}, u32[]{:S(2)}) collective-permute-start(bf16[1,2,40,128]{3,2,1,0:T(8,128)(2,1)S(1)} %get-tuple-element.62), channel_id=1, source_target_pairs={{0,6},{1,7},{2,4},{3,5},{4,2},{5,3},{6,0},{7,1},{8,14},{9,15},{10,... | collective-permute-start | bytes 61448 | tf_op jit(solution)/shard_map/ppermute | solution.py:70
  167.4 10.6 %collective-permute-start.6 = (bf16[1,2,40,128]{3,2,1,0:T(8,128)(2,1)S(1)}, bf16[1,2,40,128]{3,2,1,0:T(8,128)(2,1)S(1)}, u32[]{:S(2)}, u32[]{:S(2)}) collective-permute-start(bf16[1,2,40,128]{3,2,1,0:T(8,128)(2,1)S(1)} %get-tuple-element.61), channel_id=1, source_target_pairs={{0,7},{1,6},{2,5},{3,4},{4,3},{5,2},{6,1},{7,0},{8,15},{9,14},{10,... | collective-permute-start | bytes 61448 | tf_op jit(solution)/shard_map/ppermute | solution.py:70
  170.1 9.7 %collective-permute-start.7 = (bf16[1,2,40,128]{3,2,1,0:T(8,128)(2,1)S(1)}, bf16[1,2,40,128]{3,2,1,0:T(8,128)(2,1)S(1)}, u32[]{:S(2)}, u32[]{:S(2)}) collective-permute-start(bf16[1,2,40,128]{3,2,1,0:T(8,128)(2,1)S(1)} %get-tuple-element.60), channel_id=1, source_target_pairs={{0,8},{1,9},{2,10},{3,11},{4,12},{5,13},{6,14},{7,15},{8,0},{9,1},... | collective-permute-start | bytes 61448 | tf_op jit(solution)/shard_map/ppermute | solution.py:70
  170.5 11.5 %collective-permute-start.8 = (bf16[1,2,40,128]{3,2,1,0:T(8,128)(2,1)S(1)}, bf16[1,2,40,128]{3,2,1,0:T(8,128)(2,1)S(1)}, u32[]{:S(2)}, u32[]{:S(2)}) collective-permute-start(bf16[1,2,40,128]{3,2,1,0:T(8,128)(2,1)S(1)} %get-tuple-element.59), channel_id=1, source_target_pairs={{0,9},{1,8},{2,11},{3,10},{4,13},{5,12},{6,15},{7,14},{8,1},{9,0},... | collective-permute-start | bytes 61448 | tf_op jit(solution)/shard_map/ppermute | solution.py:70
  173.2 11.0 %collective-permute-start.9 = (bf16[1,2,40,128]{3,2,1,0:T(8,128)(2,1)S(1)}, bf16[1,2,40,128]{3,2,1,0:T(8,128)(2,1)S(1)}, u32[]{:S(2)}, u32[]{:S(2)}) collective-permute-start(bf16[1,2,40,128]{3,2,1,0:T(8,128)(2,1)S(1)} %get-tuple-element.58), channel_id=1, source_target_pairs={{0,10},{1,11},{2,8},{3,9},{4,14},{5,15},{6,12},{7,13},{8,2},{9,3},... | collective-permute-start | bytes 61448 | tf_op jit(solution)/shard_map/ppermute | solution.py:70
  174.1 13.7 %collective-permute-start.10 = (bf16[1,2,40,128]{3,2,1,0:T(8,128)(2,1)S(1)}, bf16[1,2,40,128]{3,2,1,0:T(8,128)(2,1)S(1)}, u32[]{:S(2)}, u32[]{:S(2)}) collective-permute-start(bf16[1,2,40,128]{3,2,1,0:T(8,128)(2,1)S(1)} %get-tuple-element.57), channel_id=1, source_target_pairs={{0,11},{1,10},{2,9},{3,8},{4,15},{5,14},{6,13},{7,12},{8,3},{9,2},... | collective-permute-start | bytes 61448 | tf_op jit(solution)/shard_map/ppermute | solution.py:70
  178.1 9.8 %collective-permute-start.11 = (bf16[1,2,40,128]{3,2,1,0:T(8,128)(2,1)S(1)}, bf16[1,2,40,128]{3,2,1,0:T(8,128)(2,1)S(1)}, u32[]{:S(2)}, u32[]{:S(2)}) collective-permute-start(bf16[1,2,40,128]{3,2,1,0:T(8,128)(2,1)S(1)} %get-tuple-element.56), channel_id=1, source_target_pairs={{0,12},{1,13},{2,14},{3,15},{4,8},{5,9},{6,10},{7,11},{8,4},{9,5},... | collective-permute-start | bytes 61448 | tf_op jit(solution)/shard_map/ppermute | solution.py:70
  179.8 8.0 %collective-permute-start.12 = (bf16[1,2,40,128]{3,2,1,0:T(8,128)(2,1)S(1)}, bf16[1,2,40,128]{3,2,1,0:T(8,128)(2,1)S(1)}, u32[]{:S(2)}, u32[]{:S(2)}) collective-permute-start(bf16[1,2,40,128]{3,2,1,0:T(8,128)(2,1)S(1)} %get-tuple-element.55), channel_id=1, source_target_pairs={{0,13},{1,12},{2,15},{3,14},{4,9},{5,8},{6,11},{7,10},{8,5},{9,4},... | collective-permute-start | bytes 61448 | tf_op jit(solution)/shard_map/ppermute | solution.py:70
  182.0 6.5 %collective-permute-start.13 = (bf16[1,2,40,128]{3,2,1,0:T(8,128)(2,1)S(1)}, bf16[1,2,40,128]{3,2,1,0:T(8,128)(2,1)S(1)}, u32[]{:S(2)}, u32[]{:S(2)}) collective-permute-start(bf16[1,2,40,128]{3,2,1,0:T(8,128)(2,1)S(1)} %get-tuple-element.54), channel_id=1, source_target_pairs={{0,14},{1,15},{2,12},{3,13},{4,10},{5,11},{6,8},{7,9},{8,6},{9,7},... | collective-permute-start | bytes 61448 | tf_op jit(solution)/shard_map/ppermute | solution.py:70
  184.2 7.4 %collective-permute-start.14 = (bf16[1,2,40,128]{3,2,1,0:T(8,128)(2,1)S(1)}, bf16[1,2,40,128]{3,2,1,0:T(8,128)(2,1)S(1)}, u32[]{:S(2)}, u32[]{:S(2)}) collective-permute-start(bf16[1,2,40,128]{3,2,1,0:T(8,128)(2,1)S(1)} %get-tuple-element.53), channel_id=1, source_target_pairs={{0,15},{1,14},{2,13},{3,12},{4,11},{5,10},{6,9},{7,8},{8,7},{9,6},... | collective-permute-start | bytes 61448 | tf_op jit(solution)/shard_map/ppermute | solution.py:70
Sparse Core Ops, SparseCore 0:
  8.9 13.2 all-gather.4
  24.9 99.5 all-gather.2
